TPU v7x, 32 devices: a whole 2x2x4 slice. The times are simulated.
32 devices in a mesh: row: 4 (over z), col: 4 (over x, core), tm: 2 (over y).
Axes of the slice: x: 2, y: 2, z: 4, core: 2. Of those that a mesh axis runs over, the one named last changes fastest.
Arguments:
- samples: bfloat16 [1024, 4, 2, 16384], P('row', None, 'tm', 'col'), may hold values from -6 to 6
- whitening: bfloat16 [1024, 1024], replicated, may hold values from -0.1875 to 0.1875
- ridge: float32 [2048], P('col'), may hold values from 2 to 20
- slab_start: int32 [1], replicated, may hold values from 0 to 63
- panels: int32 [4], replicated, may hold values from 0 to 3, as said below
Outputs:
- trailing: float32 [131072, 2048], P(('row', 'tm'), 'col')
- factor: bfloat16 [2, 131072, 512], P(None, ('row', 'tm'))
Inputs may be any that keep to these rules, and one draw needn't show every extreme that they name: `panels`: each panel index once.
All inputs are finite; a program needn't handle non-finite values.
Results may differ from a plain program's by a relative error of at most 0.012.
The roundings to bfloat16 on the way count: a program that leaves them out, or rounds other values in their place, can miss the bound.
Values may be sent and summed in bfloat16 or wider, within the bound.
A program may use at most 256 MiB of HBM per device.

v0:
```python
import jax
import jax.numpy as jnp
from jax import lax
from jax.sharding import PartitionSpec as P

S = 1024
PANEL = 512
PANELS = 2


def broadcast(block, axis, holder):
    block = jnp.where(lax.axis_index(axis) == holder, block, jnp.zeros_like(block))
    return lax.psum(block, axis)


def on_device(samples, whitening, ridge, slab_start, panels):
    moved = lax.all_to_all(samples, "row", split_axis=1, concat_axis=0, tiled=True)
    local_width = moved.shape[3]
    series = moved.reshape(moved.shape[0], local_width)
    whitened = jnp.dot(whitening, series, preferred_element_type=jnp.float32).astype(jnp.bfloat16)
    col_count = lax.axis_size("col")
    tm_count = lax.axis_size("tm")
    rows_here = col_count * local_width
    slab_width = PANEL * col_count
    scale = S ** (-0.5)
    slab_first = slab_start[0] * slab_width
    owner_index = slab_first // rows_here
    slab_offset = slab_first % rows_here
    col_index = lax.axis_index("col")
    self_index = lax.axis_index("row") * tm_count + lax.axis_index("tm")
    row_series = lax.all_gather(whitened, "col", axis=1, tiled=True)
    piece = lax.dynamic_slice_in_dim(row_series, slab_offset + col_index * PANEL, PANEL, 1)
    slab_part = broadcast(piece, ("row", "tm"), owner_index)
    covariance = (
        lax.dot_general(
            row_series, slab_part, (((0,), (0,)), ((), ())), preferred_element_type=jnp.float32
        )
        * scale
    )
    owner_flag = (self_index == owner_index).astype(jnp.float32)
    ridge_rows = slab_offset + col_index * PANEL
    zero_index = jnp.zeros((), jnp.int32)
    diag_block = (
        lax.dynamic_slice(covariance, (ridge_rows, zero_index), (PANEL, PANEL))
        + jnp.diag(ridge) * owner_flag
    )
    covariance = lax.dynamic_update_slice(covariance, diag_block, (ridge_rows, zero_index))
    identity = jnp.eye(PANEL, dtype=jnp.float32)
    factors = []
    finished = col_index < 0
    for section in range(PANELS):
        panel_index = panels[section]
        finished = finished | (col_index == panel_index)
        pivot_local = lax.dynamic_slice_in_dim(
            covariance, slab_offset + panel_index * PANEL, PANEL, 0
        )
        pivot_rows = broadcast(pivot_local, ("row", "tm"), owner_index)
        pivot_safe = jnp.where(col_index == panel_index, pivot_rows, identity)
        lower_factor = jnp.linalg.cholesky(pivot_safe)
        panel_now = jax.scipy.linalg.solve_triangular(lower_factor, covariance.T, lower=True).T
        small_block = lower_factor
        panel_bf = broadcast(panel_now.astype(jnp.bfloat16), "col", panel_index)
        small_block = broadcast(small_block, "col", panel_index)
        coupling = jax.scipy.linalg.solve_triangular(small_block, pivot_rows, lower=True).T
        coupling_bf = coupling.astype(jnp.bfloat16)
        covariance = covariance - lax.dot_general(
            panel_bf, coupling_bf, (((1,), (1,)), ((), ())), preferred_element_type=jnp.float32
        )
        factors.append(panel_bf)
    trailing = jnp.where(finished, jnp.zeros_like(covariance), covariance)
    return (trailing, jnp.stack(factors))


def solution(mesh):
    in_specs = (P("row", None, "tm", "col"), P(), P("col"), P(), P())
    out_specs = (P(("row", "tm"), "col"), P(None, ("row", "tm"), None))
    return jax.shard_map(
        on_device, mesh=mesh, in_specs=in_specs, out_specs=out_specs, check_vma=False
    )
```

profile of v0, /device:TPU:0, one launch (start us, length us, event | category | flops | bytes accessed | tf_op | source)
XLA Modules:
  0.0 1940.5 jit_solution(8248852513893661534)
XLA Ops:
  18.7 189.4 %all_to_all.15 = bf16[256,4,1,4096]{3,0,2,1:T(8,128)(2,1)S(1)} all-to-all(bf16[256,4,1,4096]{3,0,2,1:T(8,128)(2,1)} %copy.58), channel_id=1, replica_groups=mesh['row'=4,'col'=4,'tm'=2] {'row'}, dimensions={1} | all-to-all | bytes 16777216 | tf_op jit(solution)/shard_map/all_to_all | solution.py:17
  219.7 200.6 %all-gather.2.cloned.1.call-done = bf16[1024,16384]{1,0:T(8,128)(2,1)} async-done(((bf16[1024,4096]{1,0:T(8,128)(2,1)}), bf16[1024,16384]{1,0:T(8,128)(2,1)}) %all-gather.2.cloned.1.call-update) | async-done | bytes 33554448 | tf_op jit(solution)/shard_map/all_gather | solution.py:31
  424.6 78.0 %all-reduce.9.cloned.1.call-done = bf16[1024,512]{1,0:T(8,128)(2,1)} async-done(((bf16[1024,512]{1,0:T(8,128)(2,1)}), bf16[1024,512]{1,0:T(8,128)(2,1)}) %all-reduce.9.cloned.1.call-update) | async-done | bytes 1048592 | tf_op jit(solution)/shard_map/psum | solution.py:13
  502.6 31.8 %convolution_multiply_fusion = f32[16384,512]{0,1:T(8,128)} fusion(bf16[1024,16384]{1,0:T(8,128)(2,1)} %all-gather.2.cloned.1.call-done, bf16[1024,512]{1,0:T(8,128)(2,1)} %all-reduce.9.cloned.1.call-done), kind=kOutput, calls=%fused_computation.12 | convolution fusion | flops 17188257792 | bytes 68157440 | tf_op jit(solution)/shard_map/dot_general | solution.py:35
  545.4 77.0 %all-reduce.11.cloned.1.call-done = f32[512,512]{0,1:T(8,128)} async-done(((f32[512,512]{0,1:T(8,128)}), f32[512,512]{0,1:T(8,128)}) %all-reduce.11.cloned.1.call-update) | async-done | bytes 1048592 | tf_op jit(solution)/shard_map/psum | solution.py:13
  717.8 39.3 %custom-call.34 = f32[4,128,128]{1,2,0:T(8,128)S(1)} custom-call(f32[4,128,128]{2,1,0:T(8,128)S(1)} %get-tuple-element.33), custom_call_target="InvertDiagBlocksLowerTriangular" | custom-call | tf_op jit(solution)/shard_map/jit(_solve_triangular)/triangular_solve | solution.py:60
  767.0 12.8 convolution_subtract_fusion.4
  789.3 16.7 convolution_subtract_fusion.3
  817.7 22.9 %fusion.15 = f32[128,16384]{1,0:T(8,128)} fusion(f32[128,16384]{1,0:T(8,128)} %fusion.96, f32[128,16384]{1,0:T(8,128)} %fusion.98, f32[128,16384]{1,0:T(8,128)} %copy-done.2, f32[512,16384]{1,0:T(8,128)} %bitcast.173, f32[512,512]{0,1:T(8,128)S(1)} %get-tuple-element.357), kind=kOutput, calls=%fused_computation.31 | convolution fusion | flops 9678356480 | bytes 42139648 | tf_op jit(solution)/shard_map/jit(_solve_triangular)/triangular_solve | solution.py:60
  851.8 17.2 fusion.21
  879.6 39.3 %custom-call.35 = f32[4,128,128]{1,2,0:T(8,128)S(1)} custom-call(f32[4,128,128]{2,1,0:T(8,128)S(1)} %get-tuple-element.34), custom_call_target="InvertDiagBlocksLowerTriangular" | custom-call | tf_op jit(solution)/shard_map/jit(_solve_triangular)/triangular_solve | solution.py:64
  923.8 234.4 %all-reduce.13.cloned.1.call-done = bf16[16384,512]{0,1:T(8,128)(2,1)} async-done(((bf16[16384,512]{0,1:T(8,128)(2,1)}), bf16[16384,512]{0,1:T(8,128)(2,1)}) %all-reduce.13.cloned.1.call-update) | async-done | bytes 16777232 | tf_op jit(solution)/shard_map/psum | solution.py:13
  1158.2 28.8 %convolution_subtract_fusion = f32[16384,512]{0,1:T(8,128)} fusion(f32[16384,512]{0,1:T(8,128)} %dynamic_update_slice.3, bf16[16384,512]{0,1:T(8,128)(2,1)} %all-reduce.13.cloned.1.call-done, bf16[128,512]{1,0:T(8,128)(2,1)S(1)} %fusion.91, f32[128,512]{1,0:T(8,128)S(1)} %fusion.92, f32[128,512]{1,0:T(8,128)S(1)} %fusion.94, f32[128,512]{1,0:T(8,128)S(1)} %fusion.60), kind=kOutput, calls=%fused_computation.25 | convolution fusion | flops 8600420352 | bytes 84803584 | tf_op jit(solution)/shard_map/dot_general | solution.py:66
  1190.5 77.5 %all-reduce.17.cloned.1.call-done = f32[512,512]{0,1:T(8,128)} async-done(((f32[512,512]{0,1:T(8,128)}), f32[512,512]{0,1:T(8,128)}) %all-reduce.17.cloned.1.call-update) | async-done | bytes 1048592 | tf_op jit(solution)/shard_map/psum | solution.py:13
  1363.9 39.3 %custom-call.39 = f32[4,128,128]{1,2,0:T(8,128)S(1)} custom-call(f32[4,128,128]{2,1,0:T(8,128)S(1)} %get-tuple-element.35), custom_call_target="InvertDiagBlocksLowerTriangular" | custom-call | tf_op jit(solution)/shard_map/jit(_solve_triangular)/triangular_solve | solution.py:60
  1435.4 16.6 convolution_subtract_fusion.1
  1463.7 22.9 %fusion.12 = f32[128,16384]{1,0:T(8,128)} fusion(f32[128,16384]{1,0:T(8,128)} %fusion.86, f32[128,16384]{1,0:T(8,128)} %fusion.88, f32[128,16384]{1,0:T(8,128)} %copy-done.3, f32[512,16384]{1,0:T(8,128)} %bitcast.169, f32[512,512]{0,1:T(8,128)S(1)} %get-tuple-element.358), kind=kOutput, calls=%fused_computation.30 | convolution fusion | flops 9678356480 | bytes 42139648 | tf_op jit(solution)/shard_map/jit(_solve_triangular)/triangular_solve | solution.py:60
  1497.8 17.2 fusion.19
  1524.7 39.5 %custom-call.40 = f32[4,128,128]{1,2,0:T(8,128)S(1)} custom-call(f32[4,128,128]{2,1,0:T(8,128)S(1)} %get-tuple-element.36), custom_call_target="InvertDiagBlocksLowerTriangular" | custom-call | tf_op jit(solution)/shard_map/jit(_solve_triangular)/triangular_solve | solution.py:64
  1569.0 234.4 %all-reduce.19.cloned.1.call-done = bf16[16384,512]{0,1:T(8,128)(2,1)} async-done(((bf16[16384,512]{0,1:T(8,128)(2,1)}), bf16[16384,512]{0,1:T(8,128)(2,1)}) %all-reduce.19.cloned.1.call-update) | async-done | bytes 16777232 | tf_op jit(solution)/shard_map/psum | solution.py:13
  1803.4 29.5 %subtract_select_fusion = f32[16384,512]{0,1:T(8,128)} fusion(f32[16384,512]{0,1:T(8,128)} %convolution_subtract_fusion, bf16[16384,512]{0,1:T(8,128)(2,1)} %all-reduce.19.cloned.1.call-done, pred[]{:T(512)S(6)} %or.26, bf16[128,512]{1,0:T(8,128)(2,1)S(1)} %fusion.81, f32[128,512]{1,0:T(8,128)S(1)} %fusion.82, f32[128,512]{1,0:T(8,128)S(1)} %fusion.84, ...), kind=kOutput, calls=%fused_computation.11 | convolution fusion | flops 8608808960 | bytes 84803584 | tf_op jit(solution)/shard_map/dot_general | solution.py:66
  1832.9 33.4 %copy.88 = f32[16384,512]{1,0:T(8,128)} copy(f32[16384,512]{0,1:T(8,128)} %subtract_select_fusion) | data formatting | bytes 67108864
  1866.3 23.0 %pad_maximum_fusion = bf16[2,16384,512]{1,2,0:T(8,128)(2,1)} fusion(bf16[1,16384,512]{1,2,0:T(8,128)(2,1)} %bitcast.175, bf16[1,16384,512]{1,2,0:T(8,128)(2,1)} %bitcast.174), kind=kLoop, calls=%fused_computation.10 | loop fusion | flops 16777216 | bytes 67108864 | tf_op jit(solution)/shard_map/stack | solution.py:71
  1889.3 44.1 %copy.89 = bf16[2,16384,512]{2,1,0:T(8,128)(2,1)} copy(bf16[2,16384,512]{1,2,0:T(8,128)(2,1)} %pad_maximum_fusion) | data formatting | bytes 67108864
  (232 shorter events, 384.9 us)
Async XLA Ops:
  7.2 200.9 %copy-start = (bf16[1024,1024]{1,0:T(8,128)(2,1)S(1)}, bf16[1024,1024]{1,0:T(8,128)(2,1)}, u32[]{:S(2)}) copy-start(bf16[1024,1024]{1,0:T(8,128)(2,1)} %param.11) | copy-start | bytes 6291460
  7.2 413.1 %all-gather.2.cloned.1.call-start = ((), (), s32[]{:S(2)}) async-start(), calls=%async_computation.1 | async-start | bytes 41943040 | tf_op jit(solution)/shard_map/all_gather | solution.py:31
  218.9 204.5 %copy-start.7 = (s32[4]{0:T(128)S(1)}, s32[4]{0:T(128)}, u32[]{:S(2)}) copy-start(s32[4]{0:T(128)} %param.14) | copy-start | bytes 52
  218.9 283.7 %all-reduce.9.cloned.1.call-start = ((), (), s32[]{:S(2)}) async-start(), calls=%async_computation.2 | async-start | bytes 2097152 | tf_op jit(solution)/shard_map/psum | solution.py:13
  423.1 199.3 %all-reduce.11.cloned.1.call-start = ((), (), s32[]{:S(2)}) async-start(), calls=%async_computation.3 | async-start | bytes 2097152 | tf_op jit(solution)/shard_map/psum | solution.py:13
  424.6 109.7 %copy-start.6 = (f32[512]{0:T(512)S(1)}, f32[512]{0:T(512)}, u32[]{:S(2)}) copy-start(f32[512]{0:T(512)} %param.12) | copy-start | bytes 6148
  544.5 325.2 %all-reduce.15.cloned.1.call-start = ((), (), s32[]{:S(2)}) async-start(), calls=%async_computation.5 | async-start | bytes 2097152 | tf_op jit(solution)/shard_map/psum | solution.py:13
  757.2 401.0 %all-reduce.13.cloned.1.call-start = ((), (), s32[]{:S(2)}) async-start(), calls=%async_computation.4 | async-start | bytes 33554432 | tf_op jit(solution)/shard_map/psum | solution.py:13
  767.0 12.8 copy-start.2
  868.9 50.0 %copy-start.4 = (f32[512,512]{0,1:T(8,128)S(1)}, f32[512,512]{0,1:T(8,128)}, u32[]{:S(2)}) copy-start(f32[512,512]{0,1:T(8,128)} %all-reduce.11.cloned.1.call-done) | copy-start | bytes 3145732
  869.0 399.0 %all-reduce.17.cloned.1.call-start = ((), (), s32[]{:S(2)}) async-start(), calls=%async_computation.6 | async-start | bytes 2097152 | tf_op jit(solution)/shard_map/psum | solution.py:13
  1189.6 325.4 %all-reduce.21.cloned.1.call-start = ((), (), s32[]{:S(2)}) async-start(), calls=%async_computation.8 | async-start | bytes 2097152 | tf_op jit(solution)/shard_map/psum | solution.py:13
  1403.2 400.1 %all-reduce.19.cloned.1.call-start = ((), (), s32[]{:S(2)}) async-start(), calls=%async_computation.7 | async-start | bytes 33554432 | tf_op jit(solution)/shard_map/psum | solution.py:13
  1413.0 12.8 copy-start.3
  1515.0 49.2 %copy-start.5 = (f32[512,512]{0,1:T(8,128)S(1)}, f32[512,512]{0,1:T(8,128)}, u32[]{:S(2)}) copy-start(f32[512,512]{0,1:T(8,128)} %all-reduce.17.cloned.1.call-done) | copy-start | bytes 3145732
  1889.3 44.1 %copy-start.1 = (bf16[1024,1024]{1,0:T(8,128)(2,1)S(1)}, bf16[1024,1024]{1,0:T(8,128)(2,1)}, u32[]{:S(2)}) copy-start(bf16[1024,1024]{1,0:T(8,128)(2,1)} %param.11) | copy-start | bytes 6291460
Sparse Core Ops, SparseCore 0:
  219.0 201.1 all-gather.1
  424.3 78.2 all-reduce.8
  544.6 77.7 all-reduce.10
  757.3 37.1 all-reduce.14
  869.1 289.0 all-reduce.12
  1189.7 78.1 all-reduce.16
  1403.4 36.2 all-reduce.20
  1515.1 288.2 all-reduce.18
where the time goes:
time: 1950 us; the launch traced here: 1940 us
  waiting for transfers between devices  902 us (46%)
  other arithmetic  389 us (20%)
  matrix products  304 us (16%)
  blocking collectives  189 us (10%)
  local copies, waits for them, and re-layouts  131 us (7%)
  between operations  23.4 us (1%)
    psum x7, waiting for transfers between devices, broadcast(): return lax.psum(block, axis)  701 us
    all_gather x1, waiting for transfers between devices, on_device(): row_series = lax.all_gather(whitened, 'col', axis=1, tiled=True)  201 us
    all_to_all x1, blocking collectives, on_device(): lax.all_to_all(samples, 'row', split_axis=1, concat_axis=0, tiled=True)  189 us
    another operation x14, matrix products, on_device(): jax.scipy.linalg.solve_triangular(lower_factor, covariance.T, lower=True)  189 us
    another operation x29, other arithmetic, on_device(): lower_factor = jnp.linalg.cholesky(pivot_safe)  159 us
    unnamed x19, local copies, waits for them, and re-layouts  89.1 us
    another operation x4, other arithmetic, on_device(): jax.scipy.linalg.solve_triangular(small_block, pivot_rows, lower=True)  81.5 us
    another operation x3, other arithmetic, on_device(): jax.scipy.linalg.solve_triangular(lower_factor, covariance.T, lower=True)  78.6 us
  transfers between devices with their start and end apart: 8, of which 6 were waited for; matrix products, arithmetic and copies ran while one was open for 17% of the time, Pallas kernels for 0%

commit v1 on v0

--- a/solution.py
+++ b/solution.py
@@ -8,13 +8,20 @@
 PANELS = 2
 
 
+def refer_knots(z_in, axis_key):
+    view_out = jnp.stack(jnp.split(z_in, lax.axis_size(axis_key), 1), 0)
+    r2 = lax.all_to_all(view_out, axis_key, 0, 0)
+    d_next = jnp.concatenate(r2, 0)
+    return d_next
+
+
 def broadcast(block, axis, holder):
     block = jnp.where(lax.axis_index(axis) == holder, block, jnp.zeros_like(block))
     return lax.psum(block, axis)
 
 
 def on_device(samples, whitening, ridge, slab_start, panels):
-    moved = lax.all_to_all(samples, "row", split_axis=1, concat_axis=0, tiled=True)
+    moved = refer_knots(samples, "row")
     local_width = moved.shape[3]
     series = moved.reshape(moved.shape[0], local_width)
     whitened = jnp.dot(whitening, series, preferred_element_type=jnp.float32).astype(jnp.bfloat16)

time: 1950 us -> 1970 us (1.010)
  local copies, waits for them, and re-layouts: 131 us -> 156 us
    split x0 -> x1, local copies, waits for them, and re-layouts: none -> 26.7 us  [refer_knots(): view_out = jnp.stack(jnp.split(z_in, lax.axis_size(axis_key), 1), 0)]
    unnamed x19 -> x18, local copies, waits for them, and re-layouts: 89.1 us -> 77.6 us
    another operation x29 -> x30, other arithmetic: 159 us -> 159 us  [on_device(): lower_factor = jnp.linalg.cholesky(pivot_safe)]
where the time goes in v1:
time: 1970 us
  waiting for transfers between devices  903 us (46%)
  other arithmetic  391 us (20%)
  matrix products  304 us (15%)
  blocking collectives  189 us (10%)
  local copies, waits for them, and re-layouts  156 us (8%)
  between operations  23.4 us (1%)
    psum x7, waiting for transfers between devices, broadcast(): return lax.psum(block, axis)  702 us
    all_gather x1, waiting for transfers between devices, on_device(): row_series = lax.all_gather(whitened, 'col', axis=1, tiled=True)  201 us
    all_to_all x1, blocking collectives, refer_knots(): r2 = lax.all_to_all(view_out, axis_key, 0, 0)  189 us
    another operation x14, matrix products, on_device(): jax.scipy.linalg.solve_triangular(lower_factor, covariance.T, lower=True)  189 us
    another operation x30, other arithmetic, on_device(): lower_factor = jnp.linalg.cholesky(pivot_safe)  159 us
    another operation x4, other arithmetic, on_device(): jax.scipy.linalg.solve_triangular(small_block, pivot_rows, lower=True)  81.5 us
    another operation x3, other arithmetic, on_device(): jax.scipy.linalg.solve_triangular(lower_factor, covariance.T, lower=True)  78.6 us
    unnamed x18, local copies, waits for them, and re-layouts  77.6 us
  transfers between devices with their start and end apart: 8, of which 6 were waited for; matrix products, arithmetic and copies ran while one was open for 17% of the time, Pallas kernels for 0%

profile of v1, /device:TPU:0, one launch (start us, length us, event | category | flops | bytes accessed | tf_op | source)
XLA Modules:
  0.0 1967.6 jit_solution(542598669186948439)
XLA Ops:
  7.2 26.7 %fusion.121 = (bf16[256,1,1,4096]{3,1,2,0:T(2,128)(2,1)S(1)}, bf16[256,1,1,4096]{3,1,2,0:T(2,128)(2,1)S(1)}, bf16[256,1,1,4096]{3,1,2,0:T(2,128)(2,1)S(1)}, bf16[256,1,1,4096]{3,1,2,0:T(2,128)(2,1)S(1)}) fusion(bf16[256,4,1,4096]{3,1,2,0:T(4,128)(2,1)} %param.10), kind=kLoop, calls=%fused_computation.219 | loop fusion | bytes 16777216 | tf_op jit(solution)/shard_map/split | solution.py:12
  44.6 189.3 %all_to_all.5 = bf16[4,256,1,1,4096]{4,1,3,2,0:T(8,128)(2,1)S(1)} all-to-all(bf16[4,256,1,1,4096]{4,1,3,2,0:T(8,128)(2,1)S(1)} %pad_maximum_fusion.1), channel_id=1, replica_groups=mesh['row'=4,'col'=4,'tm'=2] {'row'}, dimensions={0} | all-to-all | bytes 16777216 | tf_op jit(solution)/shard_map/all_to_all | solution.py:13
  245.9 200.6 %all-gather.2.cloned.1.call-done = bf16[1024,16384]{0,1:T(8,128)(2,1)} async-done(((bf16[1024,4096]{0,1:T(8,128)(2,1)}), bf16[1024,16384]{0,1:T(8,128)(2,1)}) %all-gather.2.cloned.1.call-update) | async-done | bytes 33554448 | tf_op jit(solution)/shard_map/all_gather | solution.py:38
  450.4 78.4 %all-reduce.9.cloned.1.call-done = bf16[1024,512]{0,1:T(8,128)(2,1)} async-done(((bf16[1024,512]{0,1:T(8,128)(2,1)}), bf16[1024,512]{0,1:T(8,128)(2,1)}) %all-reduce.9.cloned.1.call-update) | async-done | bytes 1048592 | tf_op jit(solution)/shard_map/psum | solution.py:20
  528.8 31.8 %convolution_multiply_fusion = f32[16384,512]{0,1:T(8,128)} fusion(bf16[1024,16384]{0,1:T(8,128)(2,1)} %all-gather.2.cloned.1.call-done, bf16[1024,512]{0,1:T(8,128)(2,1)} %all-reduce.9.cloned.1.call-done), kind=kOutput, calls=%fused_computation.12 | convolution fusion | flops 17188257792 | bytes 68157440 | tf_op jit(solution)/shard_map/dot_general | solution.py:42
  571.7 77.1 %all-reduce.11.cloned.1.call-done = f32[512,512]{0,1:T(8,128)} async-done(((f32[512,512]{0,1:T(8,128)}), f32[512,512]{0,1:T(8,128)}) %all-reduce.11.cloned.1.call-update) | async-done | bytes 1048592 | tf_op jit(solution)/shard_map/psum | solution.py:20
  744.8 39.3 %custom-call.34 = f32[4,128,128]{1,2,0:T(8,128)S(1)} custom-call(f32[4,128,128]{2,1,0:T(8,128)S(1)} %get-tuple-element.33), custom_call_target="InvertDiagBlocksLowerTriangular" | custom-call | tf_op jit(solution)/shard_map/jit(_solve_triangular)/triangular_solve | solution.py:67
  816.3 16.7 convolution_subtract_fusion.3
  844.7 22.9 %fusion.15 = f32[128,16384]{1,0:T(8,128)} fusion(f32[128,16384]{1,0:T(8,128)} %fusion.96, f32[128,16384]{1,0:T(8,128)} %fusion.98, f32[128,16384]{1,0:T(8,128)} %copy-done.2, f32[512,16384]{1,0:T(8,128)} %bitcast.179, f32[512,512]{0,1:T(8,128)S(1)} %get-tuple-element.345), kind=kOutput, calls=%fused_computation.31 | convolution fusion | flops 9678356480 | bytes 42139648 | tf_op jit(solution)/shard_map/jit(_solve_triangular)/triangular_solve | solution.py:67
  878.8 17.2 fusion.21
  906.7 39.3 %custom-call.35 = f32[4,128,128]{1,2,0:T(8,128)S(1)} custom-call(f32[4,128,128]{2,1,0:T(8,128)S(1)} %get-tuple-element.34), custom_call_target="InvertDiagBlocksLowerTriangular" | custom-call | tf_op jit(solution)/shard_map/jit(_solve_triangular)/triangular_solve | solution.py:71
  950.8 234.4 %all-reduce.13.cloned.1.call-done = bf16[16384,512]{0,1:T(8,128)(2,1)} async-done(((bf16[16384,512]{0,1:T(8,128)(2,1)}), bf16[16384,512]{0,1:T(8,128)(2,1)}) %all-reduce.13.cloned.1.call-update) | async-done | bytes 16777232 | tf_op jit(solution)/shard_map/psum | solution.py:20
  1185.2 28.8 %convolution_subtract_fusion = f32[16384,512]{0,1:T(8,128)} fusion(f32[16384,512]{0,1:T(8,128)} %dynamic_update_slice.3, bf16[16384,512]{0,1:T(8,128)(2,1)} %all-reduce.13.cloned.1.call-done, bf16[128,512]{1,0:T(8,128)(2,1)S(1)} %fusion.91, f32[128,512]{1,0:T(8,128)S(1)} %fusion.92, f32[128,512]{1,0:T(8,128)S(1)} %fusion.94, f32[128,512]{1,0:T(8,128)S(1)} %fusion.60), kind=kOutput, calls=%fused_computation.25 | convolution fusion | flops 8600420352 | bytes 84803584 | tf_op jit(solution)/shard_map/dot_general | solution.py:73
  1217.5 77.6 %all-reduce.17.cloned.1.call-done = f32[512,512]{0,1:T(8,128)} async-done(((f32[512,512]{0,1:T(8,128)}), f32[512,512]{0,1:T(8,128)}) %all-reduce.17.cloned.1.call-update) | async-done | bytes 1048592 | tf_op jit(solution)/shard_map/psum | solution.py:20
  1391.0 39.3 %custom-call.39 = f32[4,128,128]{1,2,0:T(8,128)S(1)} custom-call(f32[4,128,128]{2,1,0:T(8,128)S(1)} %get-tuple-element.35), custom_call_target="InvertDiagBlocksLowerTriangular" | custom-call | tf_op jit(solution)/shard_map/jit(_solve_triangular)/triangular_solve | solution.py:67
  1462.5 16.6 convolution_subtract_fusion.1
  1490.8 22.9 %fusion.12 = f32[128,16384]{1,0:T(8,128)} fusion(f32[128,16384]{1,0:T(8,128)} %fusion.86, f32[128,16384]{1,0:T(8,128)} %fusion.88, f32[128,16384]{1,0:T(8,128)} %copy-done.3, f32[512,16384]{1,0:T(8,128)} %bitcast.175, f32[512,512]{0,1:T(8,128)S(1)} %get-tuple-element.346), kind=kOutput, calls=%fused_computation.30 | convolution fusion | flops 9678356480 | bytes 42139648 | tf_op jit(solution)/shard_map/jit(_solve_triangular)/triangular_solve | solution.py:67
  1524.9 17.2 fusion.19
  1551.8 39.5 %custom-call.40 = f32[4,128,128]{1,2,0:T(8,128)S(1)} custom-call(f32[4,128,128]{2,1,0:T(8,128)S(1)} %get-tuple-element.36), custom_call_target="InvertDiagBlocksLowerTriangular" | custom-call | tf_op jit(solution)/shard_map/jit(_solve_triangular)/triangular_solve | solution.py:71
  1596.1 234.4 %all-reduce.19.cloned.1.call-done = bf16[16384,512]{0,1:T(8,128)(2,1)} async-done(((bf16[16384,512]{0,1:T(8,128)(2,1)}), bf16[16384,512]{0,1:T(8,128)(2,1)}) %all-reduce.19.cloned.1.call-update) | async-done | bytes 16777232 | tf_op jit(solution)/shard_map/psum | solution.py:20
  1830.5 29.5 %subtract_select_fusion = f32[16384,512]{0,1:T(8,128)} fusion(f32[16384,512]{0,1:T(8,128)} %convolution_subtract_fusion, bf16[16384,512]{0,1:T(8,128)(2,1)} %all-reduce.19.cloned.1.call-done, pred[]{:T(512)S(6)} %or.26, bf16[128,512]{1,0:T(8,128)(2,1)S(1)} %fusion.81, f32[128,512]{1,0:T(8,128)S(1)} %fusion.82, f32[128,512]{1,0:T(8,128)S(1)} %fusion.84, ...), kind=kOutput, calls=%fused_computation.11 | convolution fusion | flops 8608808960 | bytes 84803584 | tf_op jit(solution)/shard_map/dot_general | solution.py:73
  1860.0 33.4 %copy.62 = f32[16384,512]{1,0:T(8,128)} copy(f32[16384,512]{0,1:T(8,128)} %subtract_select_fusion) | data formatting | bytes 67108864
  1893.4 23.0 %pad_maximum_fusion = bf16[2,16384,512]{1,2,0:T(8,128)(2,1)} fusion(bf16[1,16384,512]{1,2,0:T(8,128)(2,1)} %bitcast.181, bf16[1,16384,512]{1,2,0:T(8,128)(2,1)} %bitcast.180), kind=kLoop, calls=%fused_computation.10 | loop fusion | flops 16777216 | bytes 67108864 | tf_op jit(solution)/shard_map/stack | solution.py:78
  1916.4 44.1 %copy.63 = bf16[2,16384,512]{2,1,0:T(8,128)(2,1)} copy(bf16[2,16384,512]{1,2,0:T(8,128)(2,1)} %pad_maximum_fusion) | data formatting | bytes 67108864
  (236 shorter events, 397.4 us)
Async XLA Ops:
  7.2 226.8 %copy-start = (bf16[1024,1024]{1,0:T(8,128)(2,1)S(1)}, bf16[1024,1024]{1,0:T(8,128)(2,1)}, u32[]{:S(2)}) copy-start(bf16[1024,1024]{1,0:T(8,128)(2,1)} %param.11) | copy-start | bytes 6291460
  7.2 439.3 %all-gather.2.cloned.1.call-start = ((), (), s32[]{:S(2)}) async-start(), calls=%async_computation.1 | async-start | bytes 41943040 | tf_op jit(solution)/shard_map/all_gather | solution.py:38
  245.2 204.0 %copy-start.7 = (s32[4]{0:T(128)S(1)}, s32[4]{0:T(128)}, u32[]{:S(2)}) copy-start(s32[4]{0:T(128)} %param.14) | copy-start | bytes 52
  245.2 283.6 %all-reduce.9.cloned.1.call-start = ((), (), s32[]{:S(2)}) async-start(), calls=%async_computation.2 | async-start | bytes 2097152 | tf_op jit(solution)/shard_map/psum | solution.py:20
  449.1 199.7 %all-reduce.11.cloned.1.call-start = ((), (), s32[]{:S(2)}) async-start(), calls=%async_computation.3 | async-start | bytes 2097152 | tf_op jit(solution)/shard_map/psum | solution.py:20
  450.4 110.2 %copy-start.6 = (f32[512]{0:T(512)S(1)}, f32[512]{0:T(512)}, u32[]{:S(2)}) copy-start(f32[512]{0:T(512)} %param.12) | copy-start | bytes 6148
  570.7 326.0 %all-reduce.15.cloned.1.call-start = ((), (), s32[]{:S(2)}) async-start(), calls=%async_computation.5 | async-start | bytes 2097152 | tf_op jit(solution)/shard_map/psum | solution.py:20
  784.2 401.0 %all-reduce.13.cloned.1.call-start = ((), (), s32[]{:S(2)}) async-start(), calls=%async_computation.4 | async-start | bytes 33554432 | tf_op jit(solution)/shard_map/psum | solution.py:20
  794.0 12.8 copy-start.2
  895.9 50.0 %copy-start.4 = (f32[512,512]{0,1:T(8,128)S(1)}, f32[512,512]{0,1:T(8,128)}, u32[]{:S(2)}) copy-start(f32[512,512]{0,1:T(8,128)} %all-reduce.11.cloned.1.call-done) | copy-start | bytes 3145732
  896.0 399.1 %all-reduce.17.cloned.1.call-start = ((), (), s32[]{:S(2)}) async-start(), calls=%async_computation.6 | async-start | bytes 2097152 | tf_op jit(solution)/shard_map/psum | solution.py:20
  1216.6 325.5 %all-reduce.21.cloned.1.call-start = ((), (), s32[]{:S(2)}) async-start(), calls=%async_computation.8 | async-start | bytes 2097152 | tf_op jit(solution)/shard_map/psum | solution.py:20
  1430.3 400.1 %all-reduce.19.cloned.1.call-start = ((), (), s32[]{:S(2)}) async-start(), calls=%async_computation.7 | async-start | bytes 33554432 | tf_op jit(solution)/shard_map/psum | solution.py:20
  1440.1 12.8 copy-start.3
  1542.1 49.2 %copy-start.5 = (f32[512,512]{0,1:T(8,128)S(1)}, f32[512,512]{0,1:T(8,128)}, u32[]{:S(2)}) copy-start(f32[512,512]{0,1:T(8,128)} %all-reduce.17.cloned.1.call-done) | copy-start | bytes 3145732
  1916.4 44.1 %copy-start.1 = (bf16[1024,1024]{1,0:T(8,128)(2,1)S(1)}, bf16[1024,1024]{1,0:T(8,128)(2,1)}, u32[]{:S(2)}) copy-start(bf16[1024,1024]{1,0:T(8,128)(2,1)} %param.11) | copy-start | bytes 6291460
Sparse Core Ops, SparseCore 0:
  245.3 201.1 all-gather.1
  450.6 78.2 all-reduce.8
  570.9 77.8 all-reduce.10
  784.3 37.1 all-reduce.14
  896.1 289.0 all-reduce.12
  1216.8 78.2 all-reduce.16
  1430.5 36.2 all-reduce.20
  1542.2 288.2 all-reduce.18
